TPU v7x, 32 devices: a whole 2x2x4 slice. The times are simulated.
32 devices in a mesh: cplx: 4 (over y, core), dap: 8 (over z, x).
Axes of the slice: x: 2, y: 2, z: 4, core: 2. Of those that a mesh axis runs over, the one named last changes fastest.
Arguments:
- alignment_features: bfloat16 [64, 64, 256], P(('cplx', 'dap')), parts along dimension 0, may hold values from -6 to 6
- couple_features: bfloat16 [256, 64, 128], P(('cplx', 'dap')), parts along dimension 0, may hold values from -6 to 6
- alignment_presence: int32 [64, 64], P('cplx'), parts along dimension 0, may hold values 0 or 1
- amino_presence: int32 [256], P('cplx'), parts along dimension 0, may hold values 0 or 1
- strand_identity: int32 [256], P('cplx'), parts along dimension 0, may hold values from 0 to 3, never falling along the last dimension, each value on 1 to 32 neighbouring positions
- strand_couple_embedding: float32 [2, 128], replicated, may hold values from -4 to 4
- fourfold_input_matrix: bfloat16 [256, 1024], replicated, may hold values from -0.375 to 0.375
- heads_merge_matrix: bfloat16 [256, 256], replicated, may hold values from -1.5 to 1.5
- couple_logit_matrix: bfloat16 [128, 8], replicated, may hold values from -30 to 30
- twin_factor_matrix: bfloat16 [256, 64], replicated, may hold values from -0.375 to 0.375
- tensor_reduce_matrix: bfloat16 [1024, 128], replicated, may hold values from -0.75 to 0.75
Outputs:
- alignment_mixed: bfloat16 [64, 64, 256], P(('cplx', 'dap')), parts along dimension 0
- couple_refreshed: bfloat16 [256, 64, 128], P(('cplx', 'dap')), parts along dimension 0
There are 4 independent parts, one for each index of `cplx`. A program takes and returns all parts, laid end to end along the dimension named above; an argument that names none is the same for every part. Nothing has to cross between parts.
All inputs are finite; a program needn't handle non-finite values.
Results may differ from a plain program's by a relative error of at most 0.0075.
The roundings to bfloat16 on the way count: a program that leaves them out, or rounds other values in their place, can miss the bound.
Values may be sent and summed in bfloat16 or wider, within the bound.
No kernel may reach another device: no remote copies, remote signals or barrier semaphores. Data moves between devices by JAX's collectives and lax.ppermute only.
A program may use at most 64 MiB of HBM per device.

v0:
```python
import jax
import jax.numpy as jnp
from jax import lax
from jax.sharding import PartitionSpec as P

EPS = 1e-05


def standardize_features(x):
    x = x.astype(jnp.float32)
    center = x - jnp.mean(x, axis=-1, keepdims=True)
    spread = jnp.mean(center * center, axis=-1, keepdims=True)
    return center * lax.rsqrt(spread + EPS)


def on_device(
    alignment_features,
    couple_features,
    alignment_presence,
    amino_presence,
    strand_identity,
    strand_couple_embedding,
    fourfold_input_matrix,
    heads_merge_matrix,
    couple_logit_matrix,
    twin_factor_matrix,
    tensor_reduce_matrix,
):
    res_here = couple_features.shape[0]
    every_amino_line = couple_features.shape[1]
    device_aligned_lines = alignment_features.shape[0]
    width = twin_factor_matrix.shape[1] // 2
    head_count = couple_logit_matrix.shape[1]
    head_size = heads_merge_matrix.shape[0] // head_count
    position = lax.axis_index("dap")
    res_start = position * res_here
    seq_start = position * device_aligned_lines
    chain_here = lax.dynamic_slice_in_dim(strand_identity, res_start, res_here)
    same = (chain_here[:, None] == strand_identity[None, :]).astype(jnp.float32)[..., None]
    z_in = (
        couple_features.astype(jnp.float32)
        + (1.0 - same) * strand_couple_embedding[0]
        + same * strand_couple_embedding[1]
    )
    pair_ln = standardize_features(z_in).astype(jnp.bfloat16)
    bias_here = jnp.einsum(
        "ijc,ch->hij", pair_ln, couple_logit_matrix, preferred_element_type=jnp.float32
    ).astype(jnp.bfloat16)
    bias_all = lax.all_gather(bias_here, "dap", axis=1, tiled=True)
    presence_numeric = alignment_presence.astype(jnp.float32)
    mask_rows = lax.dynamic_slice_in_dim(presence_numeric, seq_start, device_aligned_lines, 0)
    standardized_alignment = standardize_features(alignment_features).astype(jnp.bfloat16)
    mapped_lines = jnp.dot(
        standardized_alignment.reshape(
            device_aligned_lines * every_amino_line, alignment_features.shape[2]
        ),
        fourfold_input_matrix,
        preferred_element_type=jnp.float32,
    )
    mapped_lines = mapped_lines.reshape(
        device_aligned_lines, every_amino_line, 4, head_count, head_size
    )
    asking_vectors = (mapped_lines[:, :, 0] * head_size ** (-0.5)).astype(jnp.bfloat16)
    target_vectors = mapped_lines[:, :, 1].astype(jnp.bfloat16)
    content_vectors = mapped_lines[:, :, 2].astype(jnp.bfloat16)
    sigmoid_factors = jax.nn.sigmoid(mapped_lines[:, :, 3])
    scores = jnp.einsum(
        "sihd,sjhd->shij", asking_vectors, target_vectors, preferred_element_type=jnp.float32
    )
    scores = (
        scores
        + bias_all.astype(jnp.float32)[None]
        + ((mask_rows - 1.0) * 1000000000.0)[:, None, None, :]
    )
    weights = jax.nn.softmax(scores, axis=-1).astype(jnp.bfloat16)
    context = jnp.einsum(
        "shij,sjhd->sihd", weights, content_vectors, preferred_element_type=jnp.float32
    )
    gated_values = (
        (sigmoid_factors * context)
        .astype(jnp.bfloat16)
        .reshape(device_aligned_lines * every_amino_line, head_count * head_size)
    )
    offset_lines = jnp.dot(
        gated_values, heads_merge_matrix, preferred_element_type=jnp.float32
    ).reshape(alignment_features.shape)
    alignment_mixed = (alignment_features.astype(jnp.float32) + offset_lines).astype(jnp.bfloat16)
    mask_cols = lax.dynamic_slice_in_dim(presence_numeric, res_start, res_here, 1)
    count = jnp.dot(mask_cols.T, presence_numeric, precision=lax.Precision.HIGHEST) + 1.0
    rows_ln = standardize_features(alignment_mixed).astype(jnp.bfloat16)
    twin_factor_features = jnp.einsum(
        "sjm,mk->jsk", rows_ln, twin_factor_matrix, preferred_element_type=jnp.float32
    )
    mask_t = mask_rows.T[..., None]
    left_rows = (
        (twin_factor_features[:, :, :width] * mask_t)
        .astype(jnp.bfloat16)
        .reshape(every_amino_line, device_aligned_lines * width)
    )
    right_rows = (
        (twin_factor_features[:, :, width:] * mask_t)
        .astype(jnp.bfloat16)
        .reshape(every_amino_line, device_aligned_lines * width)
    )
    left_full = lax.all_to_all(left_rows, "dap", split_axis=0, concat_axis=1, tiled=True)
    piece = lax.all_gather(right_rows, "dap", axis=1, tiled=True)
    columns = piece.shape[1]
    left_part = left_full.reshape(res_here, columns // width, width)
    right_part = piece.reshape(every_amino_line, columns // width, width)
    outer = jnp.einsum("isc,jse->ijce", left_part, right_part, preferred_element_type=jnp.float32)
    outer = outer.astype(jnp.bfloat16).reshape(res_here, every_amino_line, width * width)
    update = (
        jnp.einsum("ijk,kz->ijz", outer, tensor_reduce_matrix, preferred_element_type=jnp.float32)
        / count[..., None]
    )
    resf = amino_presence.astype(jnp.float32)
    res_local = lax.dynamic_slice_in_dim(resf, res_start, res_here)
    pair_mask = res_local[:, None] * resf[None, :]
    couple_refreshed = (z_in + pair_mask[..., None] * update).astype(jnp.bfloat16)
    return (alignment_mixed, couple_refreshed)


def solution(mesh):
    in_specs = (
        P(("cplx", "dap"), None, None),
        P(("cplx", "dap"), None, None),
        P("cplx", None),
        P("cplx"),
        P("cplx"),
        P(),
        P(),
        P(),
        P(),
        P(),
        P(),
    )
    out_specs = (P(("cplx", "dap"), None, None), P(("cplx", "dap"), None, None))
    return jax.shard_map(
        on_device, mesh=mesh, in_specs=in_specs, out_specs=out_specs, check_vma=False
    )
```

profile of v0, /device:TPU:0, one launch (start us, length us, event | category | flops | bytes accessed | tf_op | source)
XLA Modules:
  0.0 88.1 jit_solution(13455693065240458379)
XLA Ops:
  0.7 0.8 dynamic_slice.12
  1.4 0.7 broadcast_subtract_fusion
  2.2 0.7 compare_convert_fusion
  2.9 0.9 %convert_reduce_fusion = f32[2,64]{1,0:T(2,128)S(1)} fusion(bf16[2,64,256]{2,1,0:T(8,128)(2,1)} %param.11), kind=kLoop, calls=%fused_computation.35 | loop fusion | flops 65408 | bytes 66048 | tf_op jit(solution)/shard_map/reduce_sum | solution.py:11
  3.8 1.0 %fusion.24 = f32[2,64]{1,0:T(2,128)S(1)} fusion(bf16[2,64,256]{2,1,0:T(8,128)(2,1)} %param.11, f32[2,64]{1,0:T(2,128)S(1)} %broadcast_multiply_fusion.3), kind=kLoop, calls=%fused_computation.42 | loop fusion | flops 130944 | bytes 66560 | tf_op jit(solution)/shard_map/reduce_sum | solution.py:12
  4.9 0.8 slice_bitcast_fusion.5
  5.6 1.2 %fusion.19 = f32[8,64]{1,0:T(8,128)S(1)} fusion(bf16[8,64,128]{2,1,0:T(8,128)(2,1)} %param.12, f32[128]{0:T(128)S(1)} %get-tuple-element.7, f32[8,64]{1,0:T(8,128)S(1)} %compare_convert_fusion, f32[128]{0:T(128)S(1)} %get-tuple-element.6, f32[8,64]{1,0:T(8,128)S(1)} %broadcast_subtract_fusion), kind=kLoop, calls=%fused_computation.33 | loop fusion | flops 392704 | bytes 138240 | tf_op jit(solution)/shard_map/reduce_sum | solution.py:11
  6.9 1.3 %multiply_reduce_fusion = f32[8,64]{1,0:T(8,128)S(1)} fusion(bf16[8,64,128]{2,1,0:T(8,128)(2,1)} %param.12, f32[8,64]{1,0:T(8,128)S(1)} %broadcast_multiply_fusion.1, f32[128]{0:T(128)S(1)} %get-tuple-element.7, f32[8,64]{1,0:T(8,128)S(1)} %compare_convert_fusion, f32[128]{0:T(128)S(1)} %get-tuple-element.6, f32[8,64]{1,0:T(8,128)S(1)} %broadcast_subtract_fusion), kind=kLoop, calls=%fused_computation.30 | loop fusion | flops 523776 | bytes 140288 | tf_op jit(solution)/shard_map/reduce_sum | solution.py:12
  8.2 0.7 convert_element_type.94
  8.9 1.4 %fusion.10 = bf16[8,8,64]{2,0,1:T(8,128)(2,1)S(1)} fusion(bf16[8,64,128]{2,1,0:T(8,128)(2,1)} %param.12, f32[8,64]{1,0:T(8,128)S(1)} %add_rsqrt_fusion, f32[8,64]{1,0:T(8,128)S(1)} %broadcast_multiply_fusion.1, f32[128]{0:T(128)S(1)} %get-tuple-element.7, f32[8,64]{1,0:T(8,128)S(1)} %compare_convert_fusion, f32[128]{0:T(128)S(1)} %get-tuple-element.6, ...), kind=kOutput, calls=%fused_computation.17 | convolution fusion | flops 1576960 | bytes 150528 | tf_op jit(solution)/shard_map/ijc,ch->hij/dot_general | solution.py:46
  10.2 32.3 %all_gather.6 = bf16[8,64,64]{2,0,1:T(8,128)(2,1)S(1)} all-gather(bf16[8,8,64]{2,0,1:T(8,128)(2,1)S(1)} %fusion.10), channel_id=1, replica_groups=mesh['cplx'=4,'dap'=8] {'dap'}, dimensions={1}, use_global_device_ids=true | all-gather | bytes 73728 | tf_op jit(solution)/shard_map/all_gather | solution.py:49
  42.6 0.1 copy.28
  42.7 1.2 %copy.27 = bf16[256,1024]{0,1:T(8,128)(2,1)S(1)} copy(bf16[256,1024]{1,0:T(8,128)(2,1)} %param.17) | data formatting | bytes 1048576 | tf_op args[6]
  44.0 0.4 fusion.49
  44.4 0.3 fusion.3
  44.7 0.1 fusion.50
  44.9 0.2 fusion.7
  45.1 0.5 copy-done.4
  45.6 0.3 convert_reduce_fusion.1
  45.9 0.2 fusion.26
  46.1 0.2 convolution_bitcast_fusion.1
  46.3 0.1 copy.31
  46.4 0.1 all_to_all.12
  46.5 0.7 reshape.178
  47.2 5.5 %all-to-all-start = ((bf16[8,2,256]{2,1,0:T(2,128)(2,1)}), bf16[8,2,256]{2,1,0:T(2,128)(2,1)S(1)}, u32[]{:S(2)}, u32[]{:S(2)}) async-start(bf16[8,2,256]{2,1,0:T(2,128)(2,1)} %reshape.178), calls=%async_computation | async-start | bytes 16384 | tf_op jit(solution)/shard_map/all_to_all | solution.py:105
  52.7 0.3 convolution_add_fusion.2
  53.1 31.1 %all_gather.7 = bf16[64,512]{0,1:T(8,128)(2,1)S(1)} all-gather(bf16[64,64]{0,1:T(8,128)(2,1)S(1)} %bitcast.75), channel_id=1, replica_groups=mesh['cplx'=4,'dap'=8] {'dap'}, dimensions={1}, use_global_device_ids=true | all-gather | bytes 73728 | tf_op jit(solution)/shard_map/all_gather | solution.py:106
  84.2 0.1 reshape.179
  84.3 0.1 reshape.175
  84.4 0.7 convert_bitcast_fusion
  85.1 1.4 %copy.34 = bf16[8,64,32,32]{1,3,2,0:T(8,128)(2,1)S(1)} copy(bf16[8,64,32,32]{1,2,0,3:T(8,128)(2,1)S(1)} %convert_bitcast_fusion) | data formatting | bytes 2097152 | tf_op jit(solution)/shard_map/convert_element_type | solution.py:111
  86.5 1.6 %fusion.8 = bf16[8,64,128]{2,1,0:T(8,128)(2,1)} fusion(bf16[8,64,1024]{1,2,0:T(8,128)(2,1)S(1)} %bitcast.72, bf16[1024,128]{1,0:T(8,128)(2,1)S(1)} %copy-done, bf16[8,64,128]{2,1,0:T(8,128)(2,1)S(1)} %copy-done.2, f32[8,64]{1,0:T(8,128)S(1)} %convolution_add_fusion.2, f32[8,64]{1,0:T(8,128)S(1)} %broadcast_multiply_fusion, f32[128]{0:T(128)S(1)} %get-tuple-element.7, ...), kind=kOutput, calls=%fused_computation.12 | convolution fusion | flops 134807552 | bytes 1582080 | tf_op jit(solution)/shard_map/ijk,kz->ijz/dot_general | solution.py:113
  (26 shorter events, 0.3 us)
Async XLA Ops:
  0.6 85.9 %copy-start = (bf16[1024,128]{1,0:T(8,128)(2,1)S(1)}, bf16[1024,128]{1,0:T(8,128)(2,1)}, u32[]{:S(2)}) copy-start(bf16[1024,128]{1,0:T(8,128)(2,1)} %param.21) | copy-start | bytes 786436
  0.6 43.3 %copy-start.1 = (bf16[2,64,256]{2,1,0:T(8,128)(2,1)S(1)}, bf16[2,64,256]{2,1,0:T(8,128)(2,1)}, u32[]{:S(2)}) copy-start(bf16[2,64,256]{2,1,0:T(8,128)(2,1)} %param.11) | copy-start | bytes 196612
  44.7 0.9 %copy-start.4 = (bf16[256,256]{1,0:T(8,128)(2,1)S(1)}, bf16[256,256]{1,0:T(8,128)(2,1)}, u32[]{:S(2)}) copy-start(bf16[256,256]{1,0:T(8,128)(2,1)} %param.18) | copy-start | bytes 393220
  44.8 1.2 %copy-start.5 = (bf16[256,64]{0,1:T(8,128)(2,1)S(1)}, bf16[256,64]{0,1:T(8,128)(2,1)}, u32[]{:S(2)}) copy-start(bf16[256,64]{0,1:T(8,128)(2,1)} %param.20) | copy-start | bytes 98308
  44.8 8.1 %copy-start.6 = (s32[64]{0:T(128)S(1)}, s32[64]{0:T(128)}, u32[]{:S(2)}) copy-start(s32[64]{0:T(128)} %param.14) | copy-start | bytes 772
  45.9 40.6 %copy-start.3 = (bf16[2,64,256]{2,1,0:T(8,128)(2,1)}, bf16[2,64,256]{2,1,0:T(8,128)(2,1)S(1)}, u32[]{:S(2)}) copy-start(bf16[2,64,256]{2,1,0:T(8,128)(2,1)S(1)} %get-tuple-element.11) | copy-start | bytes 196612
  47.2 37.0 %all-to-all-start = ((bf16[8,2,256]{2,1,0:T(2,128)(2,1)}), bf16[8,2,256]{2,1,0:T(2,128)(2,1)S(1)}, u32[]{:S(2)}, u32[]{:S(2)}) async-start(bf16[8,2,256]{2,1,0:T(2,128)(2,1)} %reshape.178), calls=%async_computation | async-start | bytes 16384 | tf_op jit(solution)/shard_map/all_to_all | solution.py:105
  85.1 1.4 %copy-start.2 = (bf16[8,64,128]{2,1,0:T(8,128)(2,1)S(1)}, bf16[8,64,128]{2,1,0:T(8,128)(2,1)}, u32[]{:S(2)}) copy-start(bf16[8,64,128]{2,1,0:T(8,128)(2,1)} %param.12) | copy-start | bytes 393220
where the time goes:
time: 88.6 us; the launch traced here: 88.1 us
  blocking collectives  63.4 us (72%)
  other arithmetic  7.06 us (8%)
  local copies, waits for them, and re-layouts  5.95 us (7%)
  starting transfers between devices  5.47 us (6%)
  matrix products  5.34 us (6%)
    all_gather x1, blocking collectives, on_device(): bias_all = lax.all_gather(bias_here, 'dap', axis=1, tiled=True)  32.3 us
    all_gather x1, blocking collectives, on_device(): piece = lax.all_gather(right_rows, 'dap', axis=1, tiled=True)  31.1 us
    all_to_all x1, starting transfers between devices, on_device(): lax.all_to_all(left_rows, 'dap', split_axis=0, concat_axis=1, tiled=True)  5.47 us
    unnamed x17, local copies, waits for them, and re-layouts  2.54 us
    reduce_sum x3, other arithmetic, standardize_features(): spread = jnp.mean(center * center, axis=-1, keepdims=True)  2.46 us
    reduce_sum x2, other arithmetic, standardize_features(): center = x - jnp.mean(x, axis=-1, keepdims=True)  2.16 us
  transfers between devices with their start and end apart: 1, of which 0 were waited for; matrix products, arithmetic and copies ran while one was open for 0% of the time, Pallas kernels for 0%

commit v1 on v0

--- a/solution.py
+++ b/solution.py
@@ -4,6 +4,12 @@
 from jax.sharding import PartitionSpec as P
 
 EPS = 1e-05
+
+
+def gather_by_exchange(x, axis, dim):
+    peers = lax.axis_size(axis)
+    repeats = [peers if d == dim else 1 for d in range(x.ndim)]
+    return lax.all_to_all(jnp.tile(x, repeats), axis, split_axis=dim, concat_axis=dim, tiled=True)
 
 
 def standardize_features(x):
@@ -46,7 +52,7 @@
     bias_here = jnp.einsum(
         "ijc,ch->hij", pair_ln, couple_logit_matrix, preferred_element_type=jnp.float32
     ).astype(jnp.bfloat16)
-    bias_all = lax.all_gather(bias_here, "dap", axis=1, tiled=True)
+    bias_all = gather_by_exchange(bias_here, "dap", 1)
     presence_numeric = alignment_presence.astype(jnp.float32)
     mask_rows = lax.dynamic_slice_in_dim(presence_numeric, seq_start, device_aligned_lines, 0)
     standardized_alignment = standardize_features(alignment_features).astype(jnp.bfloat16)

time: 88.6 us -> 65.3 us (0.74)
  blocking collectives: 63.4 us -> 31 us
  starting transfers between devices: 5.47 us -> 10.6 us
  waiting for transfers between devices: 0.01 us -> 3.33 us
    all_gather x1 -> x0, blocking collectives: 32.3 us -> none  [on_device(): bias_all = lax.all_gather(bias_here, 'dap', axis=1, tiled=True)]
    all_to_all x0 -> x1, starting transfers between devices: none -> 7.28 us  [gather_by_exchange(): lax.all_to_all(jnp.tile(x, repeats), axis, split_axis=dim, concat_axis=di...]
    all_to_all x0 -> x1, waiting for transfers between devices: none -> 3.33 us  [gather_by_exchange(): lax.all_to_all(jnp.tile(x, repeats), axis, split_axis=dim, concat_axis=di...]
    all_to_all x1, starting transfers between devices: 5.47 us -> 3.33 us  [on_device(): lax.all_to_all(left_rows, 'dap', split_axis=0, concat_axis=1, tiled=True)]
    unnamed x17 -> x19, local copies, waits for them, and re-layouts: 2.54 us -> 2.44 us
  transfers between devices with their start and end apart: 1 -> 2, of which waited for: 0 -> 1; matrix products, arithmetic and copies ran while one was open for 0% -> 5% of each run, Pallas kernels for 0% -> 0%
where the time goes in v1:
time: 65.3 us; the launch traced here: 64.8 us
  blocking collectives  31 us (47%)
  starting transfers between devices  10.6 us (16%)
  other arithmetic  7.72 us (12%)
  local copies, waits for them, and re-layouts  5.89 us (9%)
  matrix products  5.34 us (8%)
  waiting for transfers between devices  3.33 us (5%)
  between operations  0.91 us (1%)
    all_gather x1, blocking collectives, on_device(): piece = lax.all_gather(right_rows, 'dap', axis=1, tiled=True)  31 us
    all_to_all x1, starting transfers between devices, gather_by_exchange(): lax.all_to_all(jnp.tile(x, repeats), axis, split_axis=dim, concat_axis=di...  7.28 us
    all_to_all x1, starting transfers between devices, on_device(): lax.all_to_all(left_rows, 'dap', split_axis=0, concat_axis=1, tiled=True)  3.33 us
    all_to_all x1, waiting for transfers between devices, gather_by_exchange(): lax.all_to_all(jnp.tile(x, repeats), axis, split_axis=dim, concat_axis=di...  3.33 us
    reduce_sum x3, other arithmetic, standardize_features(): spread = jnp.mean(center * center, axis=-1, keepdims=True)  2.46 us
    unnamed x19, local copies, waits for them, and re-layouts  2.44 us
    reduce_sum x2, other arithmetic, standardize_features(): center = x - jnp.mean(x, axis=-1, keepdims=True)  2.16 us
    dot_general x1, matrix products, on_device(): jnp.einsum('ijk,kz->ijz', outer, tensor_reduce_matrix, preferred_element_...  1.55 us
  transfers between devices with their start and end apart: 2, of which 1 were waited for; matrix products, arithmetic and copies ran while one was open for 5% of the time, Pallas kernels for 0%

profile of v1, /device:TPU:0, one launch (start us, length us, event | category | flops | bytes accessed | tf_op | source)
XLA Modules:
  0.0 64.8 jit_solution(12735926835115421875)
XLA Ops:
  0.7 0.7 %convert_element_type.98 = f32[64]{0:T(128)S(1)} convert(s32[64]{0:T(128)} %param.14) | non-fusion elementwise | flops 64 | bytes 512 | tf_op jit(solution)/shard_map/convert_element_type | solution.py:122
  1.4 0.7 %dynamic_slice.12 = s32[8]{0:T(128)S(1)} dynamic-slice(s32[64]{0:T(128)} %param.15, s32[]{:T(128)S(6)} %select_n.8), dynamic_slice_sizes={8} | dynamic-slice | bytes 68 | tf_op jit(solution)/shard_map/dynamic_slice | solution.py:44
  2.2 0.8 %slice_bitcast_fusion.5 = (f32[128]{0:T(128)S(1)}, f32[128]{0:T(128)S(1)}) fusion(f32[2,128]{1,0:T(2,128)} %param.16), kind=kLoop, calls=%fused_computation.77 | loop fusion | bytes 2048 | tf_op jit(solution)/shard_map/mul | solution.py:48
  3.0 0.7 %compare_convert_fusion = f32[8,64]{1,0:T(8,128)S(1)} fusion(s32[64]{0:T(128)} %param.15, s32[8]{0:T(128)S(1)} %dynamic_slice.12), kind=kLoop, calls=%fused_computation.66 | loop fusion | flops 1024 | bytes 2336 | tf_op jit(solution)/shard_map/convert_element_type | solution.py:45
  3.7 0.7 %broadcast_multiply_fusion = (f32[8,64]{1,0:T(8,128)S(1)}, f32[8,64]{1,0:T(8,128)S(1)}) fusion(f32[64]{0:T(128)S(1)} %convert_element_type.98, f32[8]{0:T(128)S(1)} %dynamic_slice.14, s32[64]{0:T(128)} %param.15, s32[8]{0:T(128)S(1)} %dynamic_slice.12), kind=kLoop, calls=%fused_computation.68 | loop fusion | flops 2048 | bytes 4672 | tf_op jit(solution)/shard_map/mul | solution.py:124
  4.4 1.2 %fusion.19 = f32[8,64]{1,0:T(8,128)S(1)} fusion(bf16[8,64,128]{2,1,0:T(8,128)(2,1)} %param.12, f32[128]{0:T(128)S(1)} %get-tuple-element.7, f32[8,64]{1,0:T(8,128)S(1)} %compare_convert_fusion, f32[128]{0:T(128)S(1)} %get-tuple-element.6, f32[8,64]{1,0:T(8,128)S(1)} %get-tuple-element.13), kind=kLoop, calls=%fused_computation.33 | loop fusion | flops 392704 | bytes 138240 | tf_op jit(solution)/shard_map/reduce_sum | solution.py:17
  5.7 1.3 %multiply_reduce_fusion = f32[8,64]{1,0:T(8,128)S(1)} fusion(bf16[8,64,128]{2,1,0:T(8,128)(2,1)} %param.12, f32[8,64]{1,0:T(8,128)S(1)} %broadcast_multiply_fusion.1, f32[128]{0:T(128)S(1)} %get-tuple-element.7, f32[8,64]{1,0:T(8,128)S(1)} %compare_convert_fusion, f32[128]{0:T(128)S(1)} %get-tuple-element.6, f32[8,64]{1,0:T(8,128)S(1)} %get-tuple-element.13), kind=kLoop, calls=%fused_computation.30 | loop fusion | flops 523776 | bytes 140288 | tf_op jit(solution)/shard_map/reduce_sum | solution.py:18
  7.0 1.4 %fusion.10 = bf16[8,8,64]{2,0,1:T(8,128)(2,1)S(1)} fusion(bf16[8,64,128]{2,1,0:T(8,128)(2,1)} %param.12, f32[8,64]{1,0:T(8,128)S(1)} %add_rsqrt_fusion, f32[8,64]{1,0:T(8,128)S(1)} %broadcast_multiply_fusion.1, f32[128]{0:T(128)S(1)} %get-tuple-element.7, f32[8,64]{1,0:T(8,128)S(1)} %compare_convert_fusion, f32[128]{0:T(128)S(1)} %get-tuple-element.6, ...), kind=kOutput, calls=%fused_computation.17 | convolution fusion | flops 1576960 | bytes 150528 | tf_op jit(solution)/shard_map/ijc,ch->hij/dot_general | solution.py:52
  8.5 0.8 %reshape.182 = bf16[8,2,2048]{2,1,0:T(2,128)(2,1)} reshape(bf16[64,8,64]{2,1,0:T(8,128)(2,1)S(1)} %bitcast.81) | data formatting | bytes 131072
  9.3 7.3 %all-to-all-start = ((bf16[8,2,2048]{2,1,0:T(2,128)(2,1)}), bf16[8,2,2048]{2,1,0:T(2,128)(2,1)S(1)}, u32[]{:S(2)}, u32[]{:S(2)}) async-start(bf16[8,2,2048]{2,1,0:T(2,128)(2,1)} %reshape.182), calls=%async_computation | async-start | bytes 131072 | tf_op jit(solution)/shard_map/all_to_all | solution.py:12
  16.5 0.9 %convert_reduce_fusion = f32[2,64]{1,0:T(2,128)S(1)} fusion(bf16[2,64,256]{2,1,0:T(8,128)(2,1)} %param.11), kind=kLoop, calls=%fused_computation.35 | loop fusion | flops 65408 | bytes 66048 | tf_op jit(solution)/shard_map/reduce_sum | solution.py:17
  17.5 1.0 %fusion.24 = f32[2,64]{1,0:T(2,128)S(1)} fusion(bf16[2,64,256]{2,1,0:T(8,128)(2,1)} %param.11, f32[2,64]{1,0:T(2,128)S(1)} %broadcast_multiply_fusion.3), kind=kLoop, calls=%fused_computation.42 | loop fusion | flops 130944 | bytes 66560 | tf_op jit(solution)/shard_map/reduce_sum | solution.py:18
  18.5 0.7 %convert_element_type.94 = f32[16,64]{1,0:T(8,128)S(1)} convert(s32[16,64]{1,0:T(8,128)} %param.13) | non-fusion elementwise | flops 1024 | bytes 8192 | tf_op jit(solution)/shard_map/convert_element_type | solution.py:56
  19.2 0.2 copy.28
  19.4 0.4 fusion.49
  19.8 0.3 convolution_add_fusion.2
  20.1 3.3 %all-to-all-done = bf16[8,2,2048]{2,1,0:T(2,128)(2,1)S(1)} async-done(((bf16[8,2,2048]{2,1,0:T(2,128)(2,1)}), bf16[8,2,2048]{2,1,0:T(2,128)(2,1)S(1)}, u32[]{:S(2)}, u32[]{:S(2)}) %all-to-all-start) | async-done | bytes 65568 | tf_op jit(solution)/shard_map/all_to_all | solution.py:12
  23.4 0.1 reshape.183
  23.6 0.1 copy.31
  23.7 0.3 fusion.3
  24.0 0.1 fusion.50
  24.2 0.2 fusion.7
  24.4 0.5 copy-done.5
  24.9 0.3 convert_reduce_fusion.1
  25.2 0.2 fusion.26
  25.4 0.2 convolution_bitcast_fusion.1
  25.9 0.7 %reshape.184 = bf16[8,2,256]{2,1,0:T(2,128)(2,1)} reshape(bf16[8,8,64]{2,1,0:T(8,128)(2,1)S(1)} %all_to_all.16) | data formatting | bytes 16384
  26.6 3.3 %all-to-all-start.1 = ((bf16[8,2,256]{2,1,0:T(2,128)(2,1)}), bf16[8,2,256]{2,1,0:T(2,128)(2,1)S(1)}, u32[]{:S(2)}, u32[]{:S(2)}) async-start(bf16[8,2,256]{2,1,0:T(2,128)(2,1)} %reshape.184), calls=%async_computation.1 | async-start | bytes 16384 | tf_op jit(solution)/shard_map/all_to_all | solution.py:111
  29.9 31.0 %all_gather.3 = bf16[64,512]{0,1:T(8,128)(2,1)S(1)} all-gather(bf16[64,64]{0,1:T(8,128)(2,1)S(1)} %bitcast.83), channel_id=1, replica_groups=mesh['cplx'=4,'dap'=8] {'dap'}, dimensions={1}, use_global_device_ids=true | all-gather | bytes 73728 | tf_op jit(solution)/shard_map/all_gather | solution.py:112
  61.1 0.7 %convert_bitcast_fusion = bf16[8,64,32,32]{1,2,0,3:T(8,128)(2,1)S(1)} fusion(bf16[8,16,32,1]{2,1,0,3:T(8,128)(2,1)S(1)} %reshape.179, bf16[64,16,32,1]{0,2,1,3:T(8,128)(2,1)S(1)} %bitcast.79), kind=kOutput, calls=%fused_computation.1 | convolution fusion | flops 17301504 | bytes 1122304 | tf_op jit(solution)/shard_map/isc,jse->ijce/dot_general | solution.py:116
  61.9 1.4 %copy.37 = bf16[8,64,32,32]{1,3,2,0:T(8,128)(2,1)S(1)} copy(bf16[8,64,32,32]{1,2,0,3:T(8,128)(2,1)S(1)} %convert_bitcast_fusion) | data formatting | bytes 2097152 | tf_op jit(solution)/shard_map/convert_element_type | solution.py:117
  63.3 1.6 %fusion.8 = bf16[8,64,128]{2,1,0:T(8,128)(2,1)} fusion(bf16[8,64,1024]{1,2,0:T(8,128)(2,1)S(1)} %bitcast.78, bf16[1024,128]{1,0:T(8,128)(2,1)S(1)} %copy-done, bf16[8,64,128]{2,1,0:T(8,128)(2,1)S(1)} %copy-done.3, f32[8,64]{1,0:T(8,128)S(1)} %convolution_add_fusion.2, f32[8,64]{1,0:T(8,128)S(1)} %get-tuple-element.12, f32[128]{0:T(128)S(1)} %get-tuple-element.7, ...), kind=kOutput, calls=%fused_computation.12 | convolution fusion | flops 134807552 | bytes 1582080 | tf_op jit(solution)/shard_map/ijk,kz->ijz/dot_general | solution.py:119
  (31 shorter events, 0.7 us)
Async XLA Ops:
  0.6 62.6 %copy-start = (bf16[1024,128]{1,0:T(8,128)(2,1)S(1)}, bf16[1024,128]{1,0:T(8,128)(2,1)}, u32[]{:S(2)}) copy-start(bf16[1024,128]{1,0:T(8,128)(2,1)} %param.21) | copy-start | bytes 786436
  0.6 18.8 %copy-start.1 = (bf16[2,64,256]{2,1,0:T(8,128)(2,1)S(1)}, bf16[2,64,256]{2,1,0:T(8,128)(2,1)}, u32[]{:S(2)}) copy-start(bf16[2,64,256]{2,1,0:T(8,128)(2,1)} %param.11) | copy-start | bytes 196612
  0.7 18.6 %copy-start.2 = (bf16[256,1024]{1,0:T(8,128)(2,1)S(1)}, bf16[256,1024]{1,0:T(8,128)(2,1)}, u32[]{:S(2)}) copy-start(bf16[256,1024]{1,0:T(8,128)(2,1)} %param.17) | copy-start | bytes 1572868
  9.3 14.2 %all-to-all-start = ((bf16[8,2,2048]{2,1,0:T(2,128)(2,1)}), bf16[8,2,2048]{2,1,0:T(2,128)(2,1)S(1)}, u32[]{:S(2)}, u32[]{:S(2)}) async-start(bf16[8,2,2048]{2,1,0:T(2,128)(2,1)} %reshape.182), calls=%async_computation | async-start | bytes 131072 | tf_op jit(solution)/shard_map/all_to_all | solution.py:12
  24.0 0.9 %copy-start.5 = (bf16[256,256]{1,0:T(8,128)(2,1)S(1)}, bf16[256,256]{1,0:T(8,128)(2,1)}, u32[]{:S(2)}) copy-start(bf16[256,256]{1,0:T(8,128)(2,1)} %param.18) | copy-start | bytes 393220
  24.2 1.2 %copy-start.6 = (bf16[256,64]{0,1:T(8,128)(2,1)S(1)}, bf16[256,64]{0,1:T(8,128)(2,1)}, u32[]{:S(2)}) copy-start(bf16[256,64]{0,1:T(8,128)(2,1)} %param.20) | copy-start | bytes 98308
  25.2 38.0 %copy-start.4 = (bf16[2,64,256]{2,1,0:T(8,128)(2,1)}, bf16[2,64,256]{2,1,0:T(8,128)(2,1)S(1)}, u32[]{:S(2)}) copy-start(bf16[2,64,256]{2,1,0:T(8,128)(2,1)S(1)} %get-tuple-element.11) | copy-start | bytes 196612
  26.6 34.3 %all-to-all-start.1 = ((bf16[8,2,256]{2,1,0:T(2,128)(2,1)}), bf16[8,2,256]{2,1,0:T(2,128)(2,1)S(1)}, u32[]{:S(2)}, u32[]{:S(2)}) async-start(bf16[8,2,256]{2,1,0:T(2,128)(2,1)} %reshape.184), calls=%async_computation.1 | async-start | bytes 16384 | tf_op jit(solution)/shard_map/all_to_all | solution.py:111
  61.8 1.4 %copy-start.3 = (bf16[8,64,128]{2,1,0:T(8,128)(2,1)S(1)}, bf16[8,64,128]{2,1,0:T(8,128)(2,1)}, u32[]{:S(2)}) copy-start(bf16[8,64,128]{2,1,0:T(8,128)(2,1)} %param.12) | copy-start | bytes 393220
